TPU v7x, 32 devices: a whole 2x2x4 slice. The times are simulated.
32 devices in a mesh: real: 2 (over x), bx: 4 (over y, core), by: 4 (over z).
Axes of the slice: x: 2, y: 2, z: 4, core: 2. Of those that a mesh axis runs over, the one named last changes fastest.
Arguments:
- current: float32 [2, 12, 3, 8, 32, 128], P('real', None, None, 'bx', 'by'), may hold values from -110 to 110
- previous: float32 [2, 12, 3, 8, 32, 128], P('real', None, None, 'bx', 'by'), may hold values from -110 to 110
- element_stiffness: float32 [24, 24], replicated, may hold values from -0.75 to 1.25, as said below
- preconditioner: float32 [2, 3, 8, 32, 128], P('real', None, 'bx', 'by'), may hold values from 0.04 to 0.16
- modulus: float32 [8, 32, 128], P('bx', 'by'), may hold values from 0.3 to 9.1
- density: float32 [8, 32, 128], P('bx', 'by'), may hold values from 0.5 to 2
- solid: int32 [2, 8, 32, 128], P('real', 'bx', 'by'), may hold values from 0 to 1, as said below
- clamped: int32 [8, 32], P('bx', 'by'), may hold values 0 or 1
Outputs:
- gram_stiff: float32 [2, 36, 36], P('real')
- gram_mass: float32 [2, 36, 36], P('real')
- search_block: float32 [2, 12, 3, 8, 32, 128], P('real', None, None, 'bx', 'by')
- sensitivity: float32 [8, 32, 128], P('bx', 'by', 'real')
Inputs may be any that keep to these rules, and one draw needn't show every extreme that they name: `element_stiffness`: symmetric positive definite: the stiffness of a trilinear brick of unit edge for unit modulus and a Poisson ratio between 0.25 and 0.35, divided by its diagonal entry, plus a small positive definite part. 1 marks a solid element of that realization; a realization's solid elements include those of every realization before it. `clamped`: 1 marks a bottom-face node held in all three directions.
All inputs are finite; a program needn't handle non-finite values. No bound on the sum of `clamped` on one device may be relied on, other than what follows from the above.
Results may differ from a plain program's by a relative error of at most 0.00013.
Values sent between devices are 32-bit elements; how exact they have to be, the bound alone decides.
No kernel may reach another device: no remote copies, remote signals or barrier semaphores. Data moves between devices by JAX's collectives and lax.ppermute only.
A program may use at most 64 MiB of HBM per device.

v0:
```python
import jax
import jax.numpy as jnp
from jax import lax
from jax.sharding import PartitionSpec as P

highest = lax.Precision.HIGHEST
soft_power = 4.0
group_width = 4
corner_list = [
    (0, 0, 0),
    (0, 0, 1),
    (0, 1, 0),
    (0, 1, 1),
    (1, 0, 0),
    (1, 0, 1),
    (1, 1, 0),
    (1, 1, 1),
]


def from_behind(value, axis, steps):
    count = lax.axis_size(axis)
    leading, last = (max(0, -steps), min(count, count - steps))
    return lax.ppermute(value, axis, [(source, source + steps) for source in range(leading, last)])


def corner_values(extended, size_x, size_y, size_z):
    return jnp.stack(
        [
            extended[
                ...,
                shift_x : shift_x + size_x,
                shift_y : shift_y + size_y,
                shift_z : shift_z + size_z,
            ]
            for shift_x, shift_y, shift_z in corner_list
        ],
        0,
    )


def scatter_corners(pieces):
    leading = pieces.ndim - 4
    overall = 0.0
    for corner, (shift_x, shift_y, shift_z) in enumerate(corner_list):
        widths = [(0, 0)] * leading + [
            (shift_x, 1 - shift_x),
            (shift_y, 1 - shift_y),
            (shift_z, 1 - shift_z),
        ]
        overall = overall + jnp.pad(pieces[corner], widths)
    return overall


def element_pass(extended, stiff_field, element_four):
    size_x, size_y, size_z = stiff_field.shape
    corner_vals = corner_values(extended, size_x, size_y, size_z)
    forces = jnp.einsum("adbe,bkexyz->akdxyz", element_four, corner_vals, precision=highest)
    energy_stiff = jnp.einsum("akdxyz,akdxyz->kxyz", corner_vals, forces, precision=highest)
    energy_mass = jnp.sum(corner_vals * corner_vals, axis=(0, 2)) * 0.125
    return (scatter_corners(forces * stiff_field), energy_stiff, energy_mass)


def grouped_pass(extended, stiff_field, element_four):
    columns = extended.shape[0]
    groups = extended.reshape((columns // group_width, group_width) + extended.shape[1:])

    def run_group(group_block):
        return element_pass(group_block, stiff_field, element_four)

    assembled, energy_stiff, energy_mass = lax.map(run_group, groups)
    return (
        assembled.reshape((columns,) + assembled.shape[2:]),
        energy_stiff.reshape((columns,) + energy_stiff.shape[2:]),
        energy_mass.reshape((columns,) + energy_mass.shape[2:]),
    )


def apply_block(block, stiff_field, free_mask, element_four):
    size_x, size_y, size_z = stiff_field.shape
    upper_rim = from_behind(block[:, :, :, 0:1], "by", -1)
    widened = jnp.concatenate([block, upper_rim], 3)
    beside = from_behind(widened[:, :, 0:1], "bx", -1)
    widened = jnp.concatenate([widened, beside], 2)
    extended = jnp.pad(widened, ((0, 0), (0, 0), (0, 0), (0, 0), (0, 1)))
    assembled, energy_stiff, energy_mass = grouped_pass(extended, stiff_field, element_four)
    assembled = assembled[..., :size_z]
    spill_first = from_behind(assembled[:, :, size_x:], "bx", 1)
    owned_part = jnp.concatenate([assembled[:, :, 0:1] + spill_first, assembled[:, :, 1:size_x]], 2)
    spill_second = from_behind(owned_part[:, :, :, size_y:], "by", 1)
    owned_part = jnp.concatenate(
        [owned_part[:, :, :, 0:1] + spill_second, owned_part[:, :, :, 1:size_y]], 3
    )
    return (owned_part * free_mask, energy_stiff, energy_mass)


def lumped_nodes(mass_rims, size_x, size_y, size_z):
    return scatter_corners(jnp.stack([mass_rims] * 8, 0))[1 : size_x + 1, 1 : size_y + 1, :size_z]


def column_dots(left_block, right_block):
    return jnp.sum(left_block * right_block, axis=(1, 2, 3, 4))


def gram_matrix(left_blocks, right_blocks):
    gram_rows = []
    for left_block in left_blocks:
        flat_left = left_block.reshape(left_block.shape[0], -1)
        gram_rows.append(
            jnp.concatenate(
                [
                    jnp.einsum(
                        "ik,jk->ij",
                        flat_left,
                        right_block.reshape(right_block.shape[0], -1),
                        precision=highest,
                    )
                    for right_block in right_blocks
                ],
                1,
            )
        )
    return jnp.concatenate(gram_rows, 0)


def shards(current, previous, element_stiffness, preconditioner, modulus, density, solid, clamped):
    element_four = element_stiffness.reshape(8, 3, 8, 3)
    size_x, size_y, size_z = modulus.shape
    columns = current.shape[1]
    dof_count = 3.0 * size_x * size_y * size_z * lax.axis_size("bx") * lax.axis_size("by")
    bottom = (jnp.arange(size_z) == 0).astype(jnp.float32)
    free_mask = 1.0 - clamped.astype(jnp.float32)[:, :, None] * bottom
    solid_share = solid[0].astype(jnp.float32)
    stiff_field = modulus * (0.02 + 0.98 * solid_share)
    mass_field = density * (0.1 + 0.9 * solid_share)
    mass_eighth = mass_field * 0.125
    below_x = from_behind(mass_eighth[size_x - 1 :], "bx", 1)
    widened_mass = jnp.concatenate([below_x, mass_eighth], 0)
    below_y = from_behind(widened_mass[:, size_y - 1 :], "by", 1)
    mass_rims = jnp.concatenate([below_y, widened_mass], 1)
    lumped_free = lumped_nodes(mass_rims, size_x, size_y, size_z) * free_mask
    current_free = current[0] * free_mask
    previous_free = previous[0] * free_mask
    stiff_pair, energy_stiff, energy_mass = apply_block(
        jnp.concatenate([current_free, previous_free], 0), stiff_field, free_mask, element_four
    )
    stiff_cur = stiff_pair[:columns]
    stiff_prev = stiff_pair[columns:]
    mass_cur = lumped_free * current_free
    mass_prev = lumped_free * previous_free
    energy_stiff = energy_stiff[:columns]
    energy_mass = energy_mass[:columns]
    scaling = preconditioner[0][None]
    numerator, denominator = lax.psum(
        (
            column_dots(current_free, stiff_cur) / dof_count,
            column_dots(current_free, mass_cur) / dof_count,
        ),
        ("bx", "by"),
    )
    quotient = numerator / denominator
    search = scaling * (stiff_cur - mass_cur * quotient[:, None, None, None, None])
    stiff_search, _, _ = apply_block(search, stiff_field, free_mask, element_four)
    mass_search = lumped_free * search
    search_basis = [current_free, search, previous_free]
    gram_stiff, gram_mass = lax.psum(
        (
            gram_matrix(search_basis, [stiff_cur, stiff_search, stiff_prev]) / dof_count,
            gram_matrix(search_basis, [mass_cur, mass_search, mass_prev]) / dof_count,
        ),
        ("bx", "by"),
    )
    powered = quotient ** (-soft_power)
    overall = lax.psum(jnp.sum(powered), "real")
    coefficient = powered / denominator
    local_terms = 3.0 * stiff_field * jnp.einsum(
        "j,jxyz->xyz", coefficient, energy_stiff, precision=highest
    ) - mass_field * jnp.einsum(
        "j,jxyz->xyz", coefficient * quotient, energy_mass, precision=highest
    )
    summed = lax.psum_scatter(local_terms, "real", scatter_dimension=2, tiled=True)
    sensitivity = summed / overall
    return (gram_stiff[None], gram_mass[None], search[None], sensitivity)


def solution(mesh):
    in_specs = (
        P("real", None, None, "bx", "by", None),
        P("real", None, None, "bx", "by", None),
        P(),
        P("real", None, "bx", "by", None),
        P("bx", "by", None),
        P("bx", "by", None),
        P("real", "bx", "by", None),
        P("bx", "by"),
    )
    out_specs = (
        P("real", None, None),
        P("real", None, None),
        P("real", None, None, "bx", "by", None),
        P("bx", "by", "real"),
    )
    return jax.shard_map(shards, mesh=mesh, in_specs=in_specs, out_specs=out_specs, check_vma=False)
```

profile of v0, /device:TPU:0, one launch (start us, length us, event | category | flops | bytes accessed | tf_op | source)
XLA Modules:
  0.0 269.4 jit_solution(3262459947060934971)
XLA Ops:
  8.0 2.4 collective-permute-start.4
  11.2 4.4 %collective-permute-start.5 = (f32[3,1,128]{2,1,0:T(1,128)S(1)}, f32[3,1,128]{2,1,0:T(1,128)S(1)}, u32[]{:S(2)}, u32[]{:S(2)}) collective-permute-start(f32[3,1,128]{2,1,0:T(1,128)S(1)} %pad_maximum_fusion.8), channel_id=1, source_target_pairs={{0,1},{1,2},{2,3},{4,5},{5,6},{6,7},{8,9},{9,10},{10,11},{12,13},{... | collective-permute-start | bytes 4616 | tf_op jit(solution)/shard_map/ppermute | solution.py:24
  19.6 5.9 %collective-permute-done = f32[24,3,2,1,128]{4,0,3,2,1:T(8,128)S(1)} collective-permute-done((f32[24,3,2,1,128]{4,0,3,2,1:T(8,128)S(1)}, f32[24,3,2,1,128]{4,0,3,2,1:T(8,128)S(1)}, u32[]{:S(2)}, u32[]{:S(2)}) %collective-permute-start) | collective-permute-done | bytes 73760 | tf_op jit(solution)/shard_map/ppermute | solution.py:24
  29.5 2.2 pad.144.clone
  31.7 45.1 %while.28 = (s32[]{:T(128)}, f32[6,4,3,3,9,129]{5,4,3,2,1,0:T(8,128)}, f32[6,4,2,8,128]{4,3,2,1,0:T(8,128)S(1)}, f32[6,4,2,8,128]{4,3,2,1,0:T(8,128)}, f32[6,4,3...) while((s32[]{:T(128)}, ...), condition=%wide.region_2.3_spmd, body=%wide.region_0.2_spmd.sunk | while | flops 57890524 | bytes 14501753 | solution.py:71
  33.9 1.7 stack.110
  41.4 1.7 stack.110
  48.9 1.7 stack.110
  56.4 1.7 stack.110
  64.0 1.7 stack.110
  71.5 1.7 stack.110
  76.8 1.7 fusion.61
  78.6 8.4 %collective-permute-start.2 = (f32[24,3,1,9,128]{4,0,3,2,1:T(8,128)S(1)}, f32[24,3,1,9,128]{4,0,3,2,1:T(8,128)S(1)}, u32[]{:S(2)}, u32[]{:S(2)}) collective-permute-start(f32[24,3,1,9,128]{4,0,3,2,1:T(8,128)S(1)} %copy.643), channel_id=1, source_target_pairs={{0,4},{4,8},{8,12},{1,5},{5,9},{9,13},{2,6},{6,10},{10,14},{3,7},{... | collective-permute-start | bytes 995336 | tf_op jit(solution)/shard_map/ppermute | solution.py:24
  87.1 1.3 convolution_bitcast_fusion.1
  88.4 1.3 convolution_bitcast_fusion.3
  89.8 1.3 convolution_bitcast_fusion.7
  91.4 3.9 %collective-permute-start.3 = (f32[24,3,2,1,128]{4,0,3,2,1:T(8,128)S(1)}, f32[24,3,2,1,128]{4,0,3,2,1:T(8,128)S(1)}, u32[]{:S(2)}, u32[]{:S(2)}) collective-permute-start(f32[24,3,2,1,128]{4,0,3,2,1:T(8,128)S(1)} %pad_maximum_fusion.5), channel_id=1, source_target_pairs={{0,1},{1,2},{2,3},{4,5},{5,6},{6,7},{8,9},{9,10},{10,11},{12,13},{... | collective-permute-start | bytes 221192 | tf_op jit(solution)/shard_map/ppermute | solution.py:24
  95.3 1.3 convolution_bitcast_fusion.9
  97.6 32.3 %all-reduce.27 = (f32[12]{0:T(128)S(1)}, f32[12]{0:T(128)S(1)}) all-reduce(f32[12]{0:T(128)S(1)} %get-tuple-element.427, f32[12]{0:T(128)S(1)} %get-tuple-element.426), channel_id=1, replica_groups=mesh['real'=2,'bx'=4,'by'=4] {'bx','by'}, use_global_device_ids=true, to_apply=%region_4.5 | all-reduce | flops 24 | bytes 192 | tf_op jit(solution)/shard_map/psum | solution.py:154
  143.0 2.8 %collective-permute-done.6 = f32[12,3,2,1,128]{4,0,3,2,1:T(8,128)S(1)} collective-permute-done((f32[12,3,2,1,128]{4,0,3,2,1:T(8,128)S(1)}, f32[12,3,2,1,128]{4,0,3,2,1:T(8,128)S(1)}, u32[]{:S(2)}, u32[]{:S(2)}) %collective-permute-start.6) | collective-permute-done | bytes 36896 | tf_op jit(solution)/shard_map/ppermute | solution.py:24
  150.1 25.6 %while.29 = (s32[]{:T(128)}, f32[3,4,3,3,9,129]{5,4,3,2,1,0:T(8,128)}, f32[3,4,3,3,9,129]{5,4,3,2,1,0:T(8,128)S(1)}, f32[8,3,8,3]{2,0,3,1:T(8,128)}, f32[2,8,128]{2,1,0:T(8,128)S(1)}, /*index=5*/s32[]{:T(128)}) while((s32[]{:T(128)}, f32[3,4,3,3,9,129]{5,4,3,2,1,0:T(8,128)}, f32[3,4,3,3,9,129]{5,4,3,2,1,0:T(8,128)S(1)}, ...), condition=%wide.region_8.9_spmd, body=%wide.region_7.8_spmd.sunk | while | flops 57112284 | bytes 15171361 | solution.py:71
  152.6 2.4 stack.111
  155.0 1.6 fusion.79
  161.1 2.4 stack.111
  163.5 1.6 fusion.79
  169.6 2.4 stack.111
  172.0 1.6 fusion.79
  175.8 1.3 fusion.62
  177.2 5.9 %collective-permute-start.8 = (f32[12,3,1,9,128]{4,0,3,2,1:T(8,128)S(1)}, f32[12,3,1,9,128]{4,0,3,2,1:T(8,128)S(1)}, u32[]{:S(2)}, u32[]{:S(2)}) collective-permute-start(f32[12,3,1,9,128]{4,0,3,2,1:T(8,128)S(1)} %copy.646), channel_id=1, source_target_pairs={{0,4},{4,8},{8,12},{1,5},{5,9},{9,13},{2,6},{6,10},{10,14},{3,7},{... | collective-permute-start | bytes 497672 | tf_op jit(solution)/shard_map/ppermute | solution.py:24
  184.9 5.5 %psum.39 = f32[]{:T(128)} all-reduce(f32[]{:T(128)} %get-tuple-element.354), channel_id=1, replica_groups=mesh['real'=2,'bx'=4,'by'=4] {'real'}, use_global_device_ids=true, to_apply=%region_13.14 | all-reduce | flops 1 | bytes 8 | tf_op jit(solution)/shard_map/psum | solution.py:174
  193.2 3.4 %collective-permute-start.9 = (f32[12,3,2,1,128]{4,0,3,2,1:T(8,128)S(1)}, f32[12,3,2,1,128]{4,0,3,2,1:T(8,128)S(1)}, u32[]{:S(2)}, u32[]{:S(2)}) collective-permute-start(f32[12,3,2,1,128]{4,0,3,2,1:T(8,128)S(1)} %pad_maximum_fusion.7), channel_id=1, source_target_pairs={{0,1},{1,2},{2,3},{4,5},{5,6},{6,7},{8,9},{9,10},{10,11},{12,13},{... | collective-permute-start | bytes 110600 | tf_op jit(solution)/shard_map/ppermute | solution.py:24
  200.5 60.8 %all-reduce.26 = (f32[1,36,36]{2,1,0:T(8,128)S(1)}, f32[1,36,36]{2,1,0:T(8,128)S(1)}) all-reduce(f32[1,36,36]{2,1,0:T(8,128)S(1)} %fusion.43, f32[1,36,36]{2,1,0:T(8,128)S(1)} %fusion.44), channel_id=1, replica_groups=mesh['real'=2,'bx'=4,'by'=4] {'bx','by'}, use_global_device_ids=true, to_apply=%region_9.10 | all-reduce | flops 2592 | bytes 20736 | tf_op jit(solution)/shard_map/psum | solution.py:166
  (317 shorter events, 84.9 us)
Async XLA Ops:
  7.2 185.0 %reduce-scatter.4.cloned.1.call-start = ((), (), s32[]{:S(2)}) async-start(), calls=%async_computation.1 | async-start | bytes 98304
  8.0 3.2 %collective-permute-start.4 = (f32[1,8,128]{2,1,0:T(8,128)S(1)}, f32[1,8,128]{2,1,0:T(8,128)S(1)}, u32[]{:S(2)}, u32[]{:S(2)}) collective-permute-start(f32[1,8,128]{2,1,0:T(8,128)S(1)} %slice.336), channel_id=1, source_target_pairs={{0,4},{4,8},{8,12},{1,5},{5,9},{9,13},{2,6},{6,10},{10,14},{3,7},{... | collective-permute-start | bytes 12296 | tf_op jit(solution)/shard_map/ppermute | solution.py:24
  11.2 15.7 %copy-start.28 = (f32[24,24]{1,0:T(8,128)S(1)}, f32[24,24]{1,0:T(8,128)}, u32[]{:S(2)}) copy-start(f32[24,24]{1,0:T(8,128)} %param.14) | copy-start | bytes 6916
  11.2 5.7 %collective-permute-start.5 = (f32[3,1,128]{2,1,0:T(1,128)S(1)}, f32[3,1,128]{2,1,0:T(1,128)S(1)}, u32[]{:S(2)}, u32[]{:S(2)}) collective-permute-start(f32[3,1,128]{2,1,0:T(1,128)S(1)} %pad_maximum_fusion.8), channel_id=1, source_target_pairs={{0,1},{1,2},{2,3},{4,5},{5,6},{6,7},{8,9},{9,10},{10,11},{12,13},{... | collective-permute-start | bytes 4616 | tf_op jit(solution)/shard_map/ppermute | solution.py:24
  17.0 10.2 %copy-start = (f32[1,12,3,2,8,128]{5,4,3,2,1,0:T(8,128)S(1)}, f32[1,12,3,2,8,128]{5,4,3,2,1,0:T(8,128)}, u32[]{:S(2)}) copy-start(f32[1,12,3,2,8,128]{5,4,3,2,1,0:T(8,128)} %param.12) | copy-start | bytes 884740
  17.0 10.2 %copy-start.1 = (f32[1,12,3,2,8,128]{5,4,3,2,1,0:T(8,128)S(1)}, f32[1,12,3,2,8,128]{5,4,3,2,1,0:T(8,128)}, u32[]{:S(2)}) copy-start(f32[1,12,3,2,8,128]{5,4,3,2,1,0:T(8,128)} %param.13) | copy-start | bytes 884740
  18.3 7.2 %collective-permute-start = (f32[24,3,2,1,128]{4,0,3,2,1:T(8,128)S(1)}, f32[24,3,2,1,128]{4,0,3,2,1:T(8,128)S(1)}, u32[]{:S(2)}, u32[]{:S(2)}) collective-permute-start(f32[24,3,2,1,128]{4,0,3,2,1:T(8,128)S(1)} %pad_maximum_fusion.6), channel_id=1, source_target_pairs={{1,0},{2,1},{3,2},{5,4},{6,5},{7,6},{9,8},{10,9},{11,10},{13,12},{... | collective-permute-start | bytes 221192 | tf_op jit(solution)/shard_map/ppermute | solution.py:24
  25.6 3.5 %collective-permute-start.1 = (f32[24,3,1,9,128]{4,0,3,2,1:T(8,128)S(1)}, f32[24,3,1,9,128]{4,0,3,2,1:T(8,128)S(1)}, u32[]{:S(2)}, u32[]{:S(2)}) collective-permute-start(f32[24,3,1,9,128]{4,0,3,2,1:T(8,128)S(1)} %pad_maximum_fusion.2), channel_id=1, source_target_pairs={{4,0},{8,4},{12,8},{5,1},{9,5},{13,9},{6,2},{10,6},{14,10},{7,3},{... | collective-permute-start | bytes 995336 | tf_op jit(solution)/shard_map/ppermute | solution.py:24
  76.8 10.3 %copy-start.5 = (f32[12,3,2,8,128]{4,3,2,1,0:T(8,128)S(1)}, f32[12,3,2,8,128]{4,3,2,1,0:T(8,128)}, u32[]{:S(2)}) copy-start(f32[12,3,2,8,128]{4,3,2,1,0:T(8,128)} %get-tuple-element.417) | copy-start | bytes 884740
  78.6 12.6 %collective-permute-start.2 = (f32[24,3,1,9,128]{4,0,3,2,1:T(8,128)S(1)}, f32[24,3,1,9,128]{4,0,3,2,1:T(8,128)S(1)}, u32[]{:S(2)}, u32[]{:S(2)}) collective-permute-start(f32[24,3,1,9,128]{4,0,3,2,1:T(8,128)S(1)} %copy.643), channel_id=1, source_target_pairs={{0,4},{4,8},{8,12},{1,5},{5,9},{9,13},{2,6},{6,10},{10,14},{3,7},{... | collective-permute-start | bytes 995336 | tf_op jit(solution)/shard_map/ppermute | solution.py:24
  91.1 5.5 %copy-start.7 = (f32[6,4,2,8,128]{4,3,2,1,0:T(8,128)S(1)}, f32[6,4,2,8,128]{4,3,2,1,0:T(8,128)}, u32[]{:S(2)}) copy-start(f32[6,4,2,8,128]{4,3,2,1,0:T(8,128)} %copy-done.6) | copy-start | bytes 589828
  91.1 5.5 %copy-start.8 = (f32[6,4,2,8,128]{4,3,2,1,0:T(8,128)S(1)}, f32[6,4,2,8,128]{4,3,2,1,0:T(8,128)}, u32[]{:S(2)}) copy-start(f32[6,4,2,8,128]{4,3,2,1,0:T(8,128)} %get-tuple-element.163) | copy-start | bytes 589828
  91.4 5.9 %collective-permute-start.3 = (f32[24,3,2,1,128]{4,0,3,2,1:T(8,128)S(1)}, f32[24,3,2,1,128]{4,0,3,2,1:T(8,128)S(1)}, u32[]{:S(2)}, u32[]{:S(2)}) collective-permute-start(f32[24,3,2,1,128]{4,0,3,2,1:T(8,128)S(1)} %pad_maximum_fusion.5), channel_id=1, source_target_pairs={{0,1},{1,2},{2,3},{4,5},{5,6},{6,7},{8,9},{9,10},{10,11},{12,13},{... | collective-permute-start | bytes 221192 | tf_op jit(solution)/shard_map/ppermute | solution.py:24
  96.6 34.0 %copy-start.27 = (f32[1,3,2,8,128]{4,3,2,1,0:T(8,128)S(1)}, f32[1,3,2,8,128]{4,3,2,1,0:T(8,128)}, u32[]{:S(2)}) copy-start(f32[1,3,2,8,128]{4,3,2,1,0:T(8,128)} %param.15) | copy-start | bytes 73732
  134.5 6.7 %copy-start.23 = (f32[2,8,128]{2,1,0:T(8,128)S(1)}, f32[2,8,128]{2,1,0:T(8,128)}, u32[]{:S(2)}) copy-start(f32[2,8,128]{2,1,0:T(8,128)} %param.17) | copy-start | bytes 24580
  134.5 6.7 %copy-start.24 = (s32[1,2,8,128]{3,2,1,0:T(8,128)S(1)}, s32[1,2,8,128]{3,2,1,0:T(8,128)}, u32[]{:S(2)}) copy-start(s32[1,2,8,128]{3,2,1,0:T(8,128)} %param.18) | copy-start | bytes 24580
  134.5 6.7 %copy-start.25 = (f32[2,8,128]{2,1,0:T(8,128)S(1)}, f32[2,8,128]{2,1,0:T(8,128)}, u32[]{:S(2)}) copy-start(f32[2,8,128]{2,1,0:T(8,128)} %param.16) | copy-start | bytes 24580
  139.9 6.0 %collective-permute-start.6 = (f32[12,3,2,1,128]{4,0,3,2,1:T(8,128)S(1)}, f32[12,3,2,1,128]{4,0,3,2,1:T(8,128)S(1)}, u32[]{:S(2)}, u32[]{:S(2)}) collective-permute-start(f32[12,3,2,1,128]{4,0,3,2,1:T(8,128)S(1)} %slice.339), channel_id=1, source_target_pairs={{1,0},{2,1},{3,2},{5,4},{6,5},{7,6},{9,8},{10,9},{11,10},{13,12},{... | collective-permute-start | bytes 110600 | tf_op jit(solution)/shard_map/ppermute | solution.py:24
  145.9 3.8 %collective-permute-start.7 = (f32[12,3,1,9,128]{4,0,3,2,1:T(8,128)S(1)}, f32[12,3,1,9,128]{4,0,3,2,1:T(8,128)S(1)}, u32[]{:S(2)}, u32[]{:S(2)}) collective-permute-start(f32[12,3,1,9,128]{4,0,3,2,1:T(8,128)S(1)} %pad_maximum_fusion.4), channel_id=1, source_target_pairs={{4,0},{8,4},{12,8},{5,1},{9,5},{13,9},{6,2},{10,6},{14,10},{7,3},{... | collective-permute-start | bytes 497672 | tf_op jit(solution)/shard_map/ppermute | solution.py:24
  175.7 8.0 %copy-start.26 = (f32[2,8,128]{2,1,0:T(8,128)S(1)}, f32[2,8,128]{2,1,0:T(8,128)}, u32[]{:S(2)}) copy-start(f32[2,8,128]{2,1,0:T(8,128)} %multiply_subtract_fusion) | copy-start | bytes 24580
  175.7 8.9 %copy-start.9 = (f32[12,12]{1,0:T(8,128)S(1)}, f32[12,12]{1,0:T(8,128)}, u32[]{:S(2)}) copy-start(f32[12,12]{1,0:T(8,128)} %convolution_bitcast_fusion.1) | copy-start | bytes 1732
  175.8 8.9 %copy-start.10 = (f32[12,12]{1,0:T(8,128)S(1)}, f32[12,12]{1,0:T(8,128)}, u32[]{:S(2)}) copy-start(f32[12,12]{1,0:T(8,128)} %convolution_bitcast_fusion.3) | copy-start | bytes 1732
  175.8 9.0 %copy-start.11 = (f32[12,12]{1,0:T(8,128)S(1)}, f32[12,12]{1,0:T(8,128)}, u32[]{:S(2)}) copy-start(f32[12,12]{1,0:T(8,128)} %convolution_bitcast_fusion.7) | copy-start | bytes 1732
  175.8 9.0 %copy-start.14 = (f32[12,12]{1,0:T(8,128)S(1)}, f32[12,12]{1,0:T(8,128)}, u32[]{:S(2)}) copy-start(f32[12,12]{1,0:T(8,128)} %convolution_bitcast_fusion.9) | copy-start | bytes 1732
  175.8 9.0 %copy-start.18 = (f32[12,12]{1,0:T(8,128)S(1)}, f32[12,12]{1,0:T(8,128)}, u32[]{:S(2)}) copy-start(f32[12,12]{1,0:T(8,128)} %convolution_bitcast_fusion.2) | copy-start | bytes 1732
  175.8 9.0 %copy-start.19 = (f32[12,12]{1,0:T(8,128)S(1)}, f32[12,12]{1,0:T(8,128)}, u32[]{:S(2)}) copy-start(f32[12,12]{1,0:T(8,128)} %convolution_bitcast_fusion.4) | copy-start | bytes 1732
  175.8 9.0 %copy-start.20 = (f32[12,12]{1,0:T(8,128)S(1)}, f32[12,12]{1,0:T(8,128)}, u32[]{:S(2)}) copy-start(f32[12,12]{1,0:T(8,128)} %convolution_bitcast_fusion.6) | copy-start | bytes 1732
  175.8 9.0 %copy-start.21 = (f32[12,12]{1,0:T(8,128)S(1)}, f32[12,12]{1,0:T(8,128)}, u32[]{:S(2)}) copy-start(f32[12,12]{1,0:T(8,128)} %convolution_bitcast_fusion.8) | copy-start | bytes 1732
  175.8 9.0 %copy-start.22 = (f32[12,12]{1,0:T(8,128)S(1)}, f32[12,12]{1,0:T(8,128)}, u32[]{:S(2)}) copy-start(f32[12,12]{1,0:T(8,128)} %convolution_bitcast_fusion.5) | copy-start | bytes 1732
  177.2 15.9 %collective-permute-start.8 = (f32[12,3,1,9,128]{4,0,3,2,1:T(8,128)S(1)}, f32[12,3,1,9,128]{4,0,3,2,1:T(8,128)S(1)}, u32[]{:S(2)}, u32[]{:S(2)}) collective-permute-start(f32[12,3,1,9,128]{4,0,3,2,1:T(8,128)S(1)} %copy.646), channel_id=1, source_target_pairs={{0,4},{4,8},{8,12},{1,5},{5,9},{9,13},{2,6},{6,10},{10,14},{3,7},{... | collective-permute-start | bytes 497672 | tf_op jit(solution)/shard_map/ppermute | solution.py:24
  193.2 5.1 %collective-permute-start.9 = (f32[12,3,2,1,128]{4,0,3,2,1:T(8,128)S(1)}, f32[12,3,2,1,128]{4,0,3,2,1:T(8,128)S(1)}, u32[]{:S(2)}, u32[]{:S(2)}) collective-permute-start(f32[12,3,2,1,128]{4,0,3,2,1:T(8,128)S(1)} %pad_maximum_fusion.7), channel_id=1, source_target_pairs={{0,1},{1,2},{2,3},{4,5},{5,6},{6,7},{8,9},{9,10},{10,11},{12,13},{... | collective-permute-start | bytes 110600 | tf_op jit(solution)/shard_map/ppermute | solution.py:24
  198.4 2.0 copy-start.13
  (12 other events, 22.0 us)
Sparse Core Ops, SparseCore 0:
  184.8 7.2 reduce-scatter.3
where the time goes:
time: 271 us; the launch traced here: 269 us
  blocking collectives  98.6 us (36%)
  local copies, waits for them, and re-layouts  53.7 us (20%)
  starting transfers between devices  33.7 us (12%)
  matrix products  30.4 us (11%)
  other arithmetic  24 us (9%)
  between operations  14.6 us (5%)
  waiting for transfers between devices  13.2 us (5%)
    psum x1, blocking collectives, shards(): lax.psum((gram_matrix(search_basis, [stiff_cur, stiff_search, stiff_prev]...  60.8 us
    ppermute x10, starting transfers between devices, from_behind(): lax.ppermute(value, axis, [(source, source + steps) for source in range(l...  33.7 us
    psum x1, blocking collectives, shards(): lax.psum((column_dots(current_free, stiff_cur) / dof_count, column_dots(c...  32.3 us
    another operation x90, local copies, waits for them, and re-layouts, corner_values(): jnp.stack([extended[..., shift_x:shift_x + size_x, shift_y:shift_y + size...  30.4 us
    dot_general x18, matrix products, gram_matrix(): jnp.einsum('ik,jk->ij', flat_left, right_block.reshape(right_block.shape[...  20.3 us
    dynamic_update_slice x15, other arithmetic, grouped_pass(): assembled, energy_stiff, energy_mass = lax.map(run_group, groups)  14.7 us
    ppermute x10, waiting for transfers between devices, from_behind(): lax.ppermute(value, axis, [(source, source + steps) for source in range(l...  12.2 us
    dot_general x9, matrix products, element_pass(): jnp.einsum('adbe,bkexyz->akdxyz', element_four, corner_vals, precision=hi...  9.7 us
  transfers between devices with their start and end apart: 11, of which 8 were waited for; matrix products, arithmetic and copies ran while one was open for 6% of the time, Pallas kernels for 0%

commit v1 on v0

--- a/solution.py
+++ b/solution.py
@@ -1,7 +1,9 @@
+import functools
 import jax
 import jax.numpy as jnp
 from jax import lax
 from jax.sharding import PartitionSpec as P
+from jax.lax import psum
 
 highest = lax.Precision.HIGHEST
 soft_power = 4.0
@@ -16,6 +18,13 @@
     (1, 1, 0),
     (1, 1, 1),
 ]
+
+
+def extend_modes(x0, bus_axis, ax_name):
+    return psum(psum(x0, bus_axis), ax_name)
+
+
+close_meshes = functools.partial(extend_modes, bus_axis="by", ax_name="bx")
 
 
 def from_behind(value, axis, steps):
@@ -151,12 +160,11 @@
     energy_stiff = energy_stiff[:columns]
     energy_mass = energy_mass[:columns]
     scaling = preconditioner[0][None]
-    numerator, denominator = lax.psum(
+    numerator, denominator = close_meshes(
         (
             column_dots(current_free, stiff_cur) / dof_count,
             column_dots(current_free, mass_cur) / dof_count,
-        ),
-        ("bx", "by"),
+        )
     )
     quotient = numerator / denominator
     search = scaling * (stiff_cur - mass_cur * quotient[:, None, None, None, None])

time: 271 us -> 256 us (0.945)
  blocking collectives: 98.6 us -> 83.5 us
    psum x1 -> x2, blocking collectives: 32.3 us -> 17.2 us  [extend_modes(): return psum(psum(x0, bus_axis), ax_name)]
where the time goes in v1:
time: 256 us; the launch traced here: 254 us
  blocking collectives  83.5 us (33%)
  local copies, waits for them, and re-layouts  53.6 us (21%)
  starting transfers between devices  33.8 us (13%)
  matrix products  30.4 us (12%)
  other arithmetic  23.4 us (9%)
  between operations  14.6 us (6%)
  waiting for transfers between devices  13.9 us (5%)
    psum x1, blocking collectives, shards(): lax.psum((gram_matrix(search_basis, [stiff_cur, stiff_search, stiff_prev]...  60.8 us
    ppermute x10, starting transfers between devices, from_behind(): lax.ppermute(value, axis, [(source, source + steps) for source in range(l...  33.7 us
    another operation x90, local copies, waits for them, and re-layouts, corner_values(): jnp.stack([extended[..., shift_x:shift_x + size_x, shift_y:shift_y + size...  30.4 us
    dot_general x18, matrix products, gram_matrix(): jnp.einsum('ik,jk->ij', flat_left, right_block.reshape(right_block.shape[...  20.3 us
    psum x2, blocking collectives, extend_modes(): return psum(psum(x0, bus_axis), ax_name)  17.2 us
    dynamic_update_slice x15, other arithmetic, grouped_pass(): assembled, energy_stiff, energy_mass = lax.map(run_group, groups)  14.8 us
    ppermute x10, waiting for transfers between devices, from_behind(): lax.ppermute(value, axis, [(source, source + steps) for source in range(l...  12.9 us
    dot_general x9, matrix products, element_pass(): jnp.einsum('adbe,bkexyz->akdxyz', element_four, corner_vals, precision=hi...  9.7 us
  transfers between devices with their start and end apart: 11, of which 8 were waited for; matrix products, arithmetic and copies ran while one was open for 6% of the time, Pallas kernels for 0%

profile of v1, /device:TPU:0, one launch (start us, length us, event | category | flops | bytes accessed | tf_op | source)
XLA Modules:
  0.0 254.4 jit_solution(9586540628312585634)
XLA Ops:
  8.0 2.4 collective-permute-start.4
  11.2 4.4 %collective-permute-start.5 = (f32[3,1,128]{2,1,0:T(1,128)S(1)}, f32[3,1,128]{2,1,0:T(1,128)S(1)}, u32[]{:S(2)}, u32[]{:S(2)}) collective-permute-start(f32[3,1,128]{2,1,0:T(1,128)S(1)} %pad_maximum_fusion.8), channel_id=1, source_target_pairs={{0,1},{1,2},{2,3},{4,5},{5,6},{6,7},{8,9},{9,10},{10,11},{12,13},{... | collective-permute-start | bytes 4616 | tf_op jit(solution)/shard_map/ppermute | solution.py:33
  19.6 5.9 %collective-permute-done = f32[24,3,2,1,128]{4,0,3,2,1:T(8,128)S(1)} collective-permute-done((f32[24,3,2,1,128]{4,0,3,2,1:T(8,128)S(1)}, f32[24,3,2,1,128]{4,0,3,2,1:T(8,128)S(1)}, u32[]{:S(2)}, u32[]{:S(2)}) %collective-permute-start) | collective-permute-done | bytes 73760 | tf_op jit(solution)/shard_map/ppermute | solution.py:33
  27.3 1.8 collective-permute-done.1
  29.5 2.2 pad.144.clone
  31.7 45.2 %while.28 = (s32[]{:T(128)}, f32[6,4,3,3,9,129]{5,4,3,2,1,0:T(8,128)}, f32[6,4,2,8,128]{4,3,2,1,0:T(8,128)}, f32[6,4,2,8,128]{4,3,2,1,0:T(8,128)}, f32[6,4,3,3,9...) while((s32[]{:T(128)}, ...), condition=%wide.region_2.3_spmd, body=%wide.region_0.2_spmd.sunk | while | flops 57890524 | bytes 14501753 | solution.py:80
  33.9 1.7 stack.110
  41.4 1.7 stack.110
  48.9 1.7 stack.110
  56.5 1.7 stack.110
  64.0 1.7 stack.110
  71.6 1.7 stack.110
  76.9 1.6 fusion.61
  78.6 8.4 %collective-permute-start.2 = (f32[24,3,1,9,128]{4,0,3,2,1:T(8,128)S(1)}, f32[24,3,1,9,128]{4,0,3,2,1:T(8,128)S(1)}, u32[]{:S(2)}, u32[]{:S(2)}) collective-permute-start(f32[24,3,1,9,128]{4,0,3,2,1:T(8,128)S(1)} %copy.643), channel_id=1, source_target_pairs={{0,4},{4,8},{8,12},{1,5},{5,9},{9,13},{2,6},{6,10},{10,14},{3,7},{... | collective-permute-start | bytes 995336 | tf_op jit(solution)/shard_map/ppermute | solution.py:33
  87.1 1.3 convolution_bitcast_fusion.1
  88.4 1.3 convolution_bitcast_fusion.3
  91.3 3.9 %collective-permute-start.3 = (f32[24,3,2,1,128]{4,0,3,2,1:T(8,128)S(1)}, f32[24,3,2,1,128]{4,0,3,2,1:T(8,128)S(1)}, u32[]{:S(2)}, u32[]{:S(2)}) collective-permute-start(f32[24,3,2,1,128]{4,0,3,2,1:T(8,128)S(1)} %pad_maximum_fusion.5), channel_id=1, source_target_pairs={{0,1},{1,2},{2,3},{4,5},{5,6},{6,7},{8,9},{9,10},{10,11},{12,13},{... | collective-permute-start | bytes 221192 | tf_op jit(solution)/shard_map/ppermute | solution.py:33
  95.3 1.3 convolution_bitcast_fusion.9
  97.6 11.3 %all-reduce.27 = (f32[12]{0:T(128)S(1)}, f32[12]{0:T(128)S(1)}) all-reduce(f32[12]{0:T(128)S(1)} %get-tuple-element.429, f32[12]{0:T(128)S(1)} %get-tuple-element.428), channel_id=1, replica_groups=mesh['real'=2,'bx'=4,'by'=4] {'by'}, use_global_device_ids=true, to_apply=%region_4.5 | all-reduce | flops 24 | bytes 192 | tf_op jit(solution)/shard_map/psum | solution.py:24
  108.9 5.9 %all-reduce.28 = (f32[12]{0:T(128)S(1)}, f32[12]{0:T(128)S(1)}) all-reduce(f32[12]{0:T(128)S(1)} %get-tuple-element.352, f32[12]{0:T(128)S(1)} %get-tuple-element.353), channel_id=1, replica_groups=mesh['real'=2,'bx'=4,'by'=4] {'bx'}, use_global_device_ids=true, to_apply=%region_5.6 | all-reduce | flops 24 | bytes 192 | tf_op jit(solution)/shard_map/psum | solution.py:24
  127.9 2.8 %collective-permute-done.6 = f32[12,3,2,1,128]{4,0,3,2,1:T(8,128)S(1)} collective-permute-done((f32[12,3,2,1,128]{4,0,3,2,1:T(8,128)S(1)}, f32[12,3,2,1,128]{4,0,3,2,1:T(8,128)S(1)}, u32[]{:S(2)}, u32[]{:S(2)}) %collective-permute-start.6) | collective-permute-done | bytes 36896 | tf_op jit(solution)/shard_map/ppermute | solution.py:33
  135.0 25.6 %while.29 = (s32[]{:T(128)}, f32[3,4,3,3,9,129]{5,4,3,2,1,0:T(8,128)}, f32[3,4,3,3,9,129]{5,4,3,2,1,0:T(8,128)S(1)}, f32[8,3,8,3]{2,0,3,1:T(8,128)}, f32[2,8,128]{2,1,0:T(8,128)S(1)}, /*index=5*/s32[]{:T(128)}) while((s32[]{:T(128)}, f32[3,4,3,3,9,129]{5,4,3,2,1,0:T(8,128)}, f32[3,4,3,3,9,129]{5,4,3,2,1,0:T(8,128)S(1)}, ...), condition=%wide.region_10.11_spmd, body=%wide.region_9.10_spmd.sunk | while | flops 57112284 | bytes 15171361 | solution.py:80
  137.4 2.4 stack.111
  139.9 1.6 fusion.79
  146.0 2.4 stack.111
  148.4 1.6 fusion.79
  154.5 2.4 stack.111
  156.9 1.6 fusion.79
  162.1 6.0 %collective-permute-start.8 = (f32[12,3,1,9,128]{4,0,3,2,1:T(8,128)S(1)}, f32[12,3,1,9,128]{4,0,3,2,1:T(8,128)S(1)}, u32[]{:S(2)}, u32[]{:S(2)}) collective-permute-start(f32[12,3,1,9,128]{4,0,3,2,1:T(8,128)S(1)} %copy.646), channel_id=1, source_target_pairs={{0,4},{4,8},{8,12},{1,5},{5,9},{9,13},{2,6},{6,10},{10,14},{3,7},{... | collective-permute-start | bytes 497672 | tf_op jit(solution)/shard_map/ppermute | solution.py:33
  169.9 5.5 %psum.55 = f32[]{:T(128)} all-reduce(f32[]{:T(128)} %get-tuple-element.356), channel_id=1, replica_groups=mesh['real'=2,'bx'=4,'by'=4] {'real'}, use_global_device_ids=true, to_apply=%region_15.16 | all-reduce | flops 1 | bytes 8 | tf_op jit(solution)/shard_map/psum | solution.py:182
  178.2 3.4 %collective-permute-start.9 = (f32[12,3,2,1,128]{4,0,3,2,1:T(8,128)S(1)}, f32[12,3,2,1,128]{4,0,3,2,1:T(8,128)S(1)}, u32[]{:S(2)}, u32[]{:S(2)}) collective-permute-start(f32[12,3,2,1,128]{4,0,3,2,1:T(8,128)S(1)} %pad_maximum_fusion.7), channel_id=1, source_target_pairs={{0,1},{1,2},{2,3},{4,5},{5,6},{6,7},{8,9},{9,10},{10,11},{12,13},{... | collective-permute-start | bytes 110600 | tf_op jit(solution)/shard_map/ppermute | solution.py:33
  185.5 60.8 %all-reduce.26 = (f32[1,36,36]{2,1,0:T(8,128)S(1)}, f32[1,36,36]{2,1,0:T(8,128)S(1)}) all-reduce(f32[1,36,36]{2,1,0:T(8,128)S(1)} %fusion.43, f32[1,36,36]{2,1,0:T(8,128)S(1)} %fusion.44), channel_id=1, replica_groups=mesh['real'=2,'bx'=4,'by'=4] {'bx','by'}, use_global_device_ids=true, to_apply=%region_11.12 | all-reduce | flops 2592 | bytes 20736 | tf_op jit(solution)/shard_map/psum | solution.py:174
  (314 shorter events, 85.9 us)
Async XLA Ops:
  7.2 170.0 %reduce-scatter.4.cloned.1.call-start = ((), (), s32[]{:S(2)}) async-start(), calls=%async_computation.1 | async-start | bytes 98304
  8.0 3.2 %collective-permute-start.4 = (f32[1,8,128]{2,1,0:T(8,128)S(1)}, f32[1,8,128]{2,1,0:T(8,128)S(1)}, u32[]{:S(2)}, u32[]{:S(2)}) collective-permute-start(f32[1,8,128]{2,1,0:T(8,128)S(1)} %slice.336), channel_id=1, source_target_pairs={{0,4},{4,8},{8,12},{1,5},{5,9},{9,13},{2,6},{6,10},{10,14},{3,7},{... | collective-permute-start | bytes 12296 | tf_op jit(solution)/shard_map/ppermute | solution.py:33
  11.2 15.7 %copy-start.26 = (f32[24,24]{1,0:T(8,128)S(1)}, f32[24,24]{1,0:T(8,128)}, u32[]{:S(2)}) copy-start(f32[24,24]{1,0:T(8,128)} %param.14) | copy-start | bytes 6916
  11.2 5.7 %collective-permute-start.5 = (f32[3,1,128]{2,1,0:T(1,128)S(1)}, f32[3,1,128]{2,1,0:T(1,128)S(1)}, u32[]{:S(2)}, u32[]{:S(2)}) collective-permute-start(f32[3,1,128]{2,1,0:T(1,128)S(1)} %pad_maximum_fusion.8), channel_id=1, source_target_pairs={{0,1},{1,2},{2,3},{4,5},{5,6},{6,7},{8,9},{9,10},{10,11},{12,13},{... | collective-permute-start | bytes 4616 | tf_op jit(solution)/shard_map/ppermute | solution.py:33
  17.0 10.2 %copy-start = (f32[1,12,3,2,8,128]{5,4,3,2,1,0:T(8,128)S(1)}, f32[1,12,3,2,8,128]{5,4,3,2,1,0:T(8,128)}, u32[]{:S(2)}) copy-start(f32[1,12,3,2,8,128]{5,4,3,2,1,0:T(8,128)} %param.12) | copy-start | bytes 884740
  17.0 10.2 %copy-start.1 = (f32[1,12,3,2,8,128]{5,4,3,2,1,0:T(8,128)S(1)}, f32[1,12,3,2,8,128]{5,4,3,2,1,0:T(8,128)}, u32[]{:S(2)}) copy-start(f32[1,12,3,2,8,128]{5,4,3,2,1,0:T(8,128)} %param.13) | copy-start | bytes 884740
  18.3 7.2 %collective-permute-start = (f32[24,3,2,1,128]{4,0,3,2,1:T(8,128)S(1)}, f32[24,3,2,1,128]{4,0,3,2,1:T(8,128)S(1)}, u32[]{:S(2)}, u32[]{:S(2)}) collective-permute-start(f32[24,3,2,1,128]{4,0,3,2,1:T(8,128)S(1)} %pad_maximum_fusion.6), channel_id=1, source_target_pairs={{1,0},{2,1},{3,2},{5,4},{6,5},{7,6},{9,8},{10,9},{11,10},{13,12},{... | collective-permute-start | bytes 221192 | tf_op jit(solution)/shard_map/ppermute | solution.py:33
  25.6 3.5 %collective-permute-start.1 = (f32[24,3,1,9,128]{4,0,3,2,1:T(8,128)S(1)}, f32[24,3,1,9,128]{4,0,3,2,1:T(8,128)S(1)}, u32[]{:S(2)}, u32[]{:S(2)}) collective-permute-start(f32[24,3,1,9,128]{4,0,3,2,1:T(8,128)S(1)} %pad_maximum_fusion.2), channel_id=1, source_target_pairs={{4,0},{8,4},{12,8},{5,1},{9,5},{13,9},{6,2},{10,6},{14,10},{7,3},{... | collective-permute-start | bytes 995336 | tf_op jit(solution)/shard_map/ppermute | solution.py:33
  78.6 12.5 %collective-permute-start.2 = (f32[24,3,1,9,128]{4,0,3,2,1:T(8,128)S(1)}, f32[24,3,1,9,128]{4,0,3,2,1:T(8,128)S(1)}, u32[]{:S(2)}, u32[]{:S(2)}) collective-permute-start(f32[24,3,1,9,128]{4,0,3,2,1:T(8,128)S(1)} %copy.643), channel_id=1, source_target_pairs={{0,4},{4,8},{8,12},{1,5},{5,9},{9,13},{2,6},{6,10},{10,14},{3,7},{... | collective-permute-start | bytes 995336 | tf_op jit(solution)/shard_map/ppermute | solution.py:33
  91.1 5.5 %copy-start.5 = (f32[6,4,2,8,128]{4,3,2,1,0:T(8,128)S(1)}, f32[6,4,2,8,128]{4,3,2,1,0:T(8,128)}, u32[]{:S(2)}) copy-start(f32[6,4,2,8,128]{4,3,2,1,0:T(8,128)} %get-tuple-element.162) | copy-start | bytes 589828
  91.1 5.5 %copy-start.6 = (f32[6,4,2,8,128]{4,3,2,1,0:T(8,128)S(1)}, f32[6,4,2,8,128]{4,3,2,1,0:T(8,128)}, u32[]{:S(2)}) copy-start(f32[6,4,2,8,128]{4,3,2,1,0:T(8,128)} %get-tuple-element.163) | copy-start | bytes 589828
  91.3 5.9 %collective-permute-start.3 = (f32[24,3,2,1,128]{4,0,3,2,1:T(8,128)S(1)}, f32[24,3,2,1,128]{4,0,3,2,1:T(8,128)S(1)}, u32[]{:S(2)}, u32[]{:S(2)}) collective-permute-start(f32[24,3,2,1,128]{4,0,3,2,1:T(8,128)S(1)} %pad_maximum_fusion.5), channel_id=1, source_target_pairs={{0,1},{1,2},{2,3},{4,5},{5,6},{6,7},{8,9},{9,10},{10,11},{12,13},{... | collective-permute-start | bytes 221192 | tf_op jit(solution)/shard_map/ppermute | solution.py:33
  96.6 18.9 %copy-start.25 = (f32[1,3,2,8,128]{4,3,2,1,0:T(8,128)S(1)}, f32[1,3,2,8,128]{4,3,2,1,0:T(8,128)}, u32[]{:S(2)}) copy-start(f32[1,3,2,8,128]{4,3,2,1,0:T(8,128)} %param.15) | copy-start | bytes 73732
  119.4 6.7 %copy-start.21 = (f32[2,8,128]{2,1,0:T(8,128)S(1)}, f32[2,8,128]{2,1,0:T(8,128)}, u32[]{:S(2)}) copy-start(f32[2,8,128]{2,1,0:T(8,128)} %param.17) | copy-start | bytes 24580
  119.4 6.7 %copy-start.22 = (s32[1,2,8,128]{3,2,1,0:T(8,128)S(1)}, s32[1,2,8,128]{3,2,1,0:T(8,128)}, u32[]{:S(2)}) copy-start(s32[1,2,8,128]{3,2,1,0:T(8,128)} %param.18) | copy-start | bytes 24580
  119.4 6.7 %copy-start.23 = (f32[2,8,128]{2,1,0:T(8,128)S(1)}, f32[2,8,128]{2,1,0:T(8,128)}, u32[]{:S(2)}) copy-start(f32[2,8,128]{2,1,0:T(8,128)} %param.16) | copy-start | bytes 24580
  124.8 6.0 %collective-permute-start.6 = (f32[12,3,2,1,128]{4,0,3,2,1:T(8,128)S(1)}, f32[12,3,2,1,128]{4,0,3,2,1:T(8,128)S(1)}, u32[]{:S(2)}, u32[]{:S(2)}) collective-permute-start(f32[12,3,2,1,128]{4,0,3,2,1:T(8,128)S(1)} %slice.339), channel_id=1, source_target_pairs={{1,0},{2,1},{3,2},{5,4},{6,5},{7,6},{9,8},{10,9},{11,10},{13,12},{... | collective-permute-start | bytes 110600 | tf_op jit(solution)/shard_map/ppermute | solution.py:33
  130.8 3.8 %collective-permute-start.7 = (f32[12,3,1,9,128]{4,0,3,2,1:T(8,128)S(1)}, f32[12,3,1,9,128]{4,0,3,2,1:T(8,128)S(1)}, u32[]{:S(2)}, u32[]{:S(2)}) collective-permute-start(f32[12,3,1,9,128]{4,0,3,2,1:T(8,128)S(1)} %pad_maximum_fusion.4), channel_id=1, source_target_pairs={{4,0},{8,4},{12,8},{5,1},{9,5},{13,9},{6,2},{10,6},{14,10},{7,3},{... | collective-permute-start | bytes 497672 | tf_op jit(solution)/shard_map/ppermute | solution.py:33
  160.6 8.1 %copy-start.24 = (f32[2,8,128]{2,1,0:T(8,128)S(1)}, f32[2,8,128]{2,1,0:T(8,128)}, u32[]{:S(2)}) copy-start(f32[2,8,128]{2,1,0:T(8,128)} %multiply_subtract_fusion) | copy-start | bytes 24580
  160.6 9.0 %copy-start.7 = (f32[12,12]{1,0:T(8,128)S(1)}, f32[12,12]{1,0:T(8,128)}, u32[]{:S(2)}) copy-start(f32[12,12]{1,0:T(8,128)} %convolution_bitcast_fusion.1) | copy-start | bytes 1732
  160.6 9.0 %copy-start.8 = (f32[12,12]{1,0:T(8,128)S(1)}, f32[12,12]{1,0:T(8,128)}, u32[]{:S(2)}) copy-start(f32[12,12]{1,0:T(8,128)} %convolution_bitcast_fusion.3) | copy-start | bytes 1732
  160.6 9.1 %copy-start.9 = (f32[12,12]{1,0:T(8,128)S(1)}, f32[12,12]{1,0:T(8,128)}, u32[]{:S(2)}) copy-start(f32[12,12]{1,0:T(8,128)} %convolution_bitcast_fusion.7) | copy-start | bytes 1732
  160.7 9.1 %copy-start.10 = (f32[12,12]{1,0:T(8,128)S(1)}, f32[12,12]{1,0:T(8,128)}, u32[]{:S(2)}) copy-start(f32[12,12]{1,0:T(8,128)} %convolution_bitcast_fusion.9) | copy-start | bytes 1732
  160.7 9.1 %copy-start.16 = (f32[12,12]{1,0:T(8,128)S(1)}, f32[12,12]{1,0:T(8,128)}, u32[]{:S(2)}) copy-start(f32[12,12]{1,0:T(8,128)} %convolution_bitcast_fusion.2) | copy-start | bytes 1732
  160.7 9.1 %copy-start.17 = (f32[12,12]{1,0:T(8,128)S(1)}, f32[12,12]{1,0:T(8,128)}, u32[]{:S(2)}) copy-start(f32[12,12]{1,0:T(8,128)} %convolution_bitcast_fusion.4) | copy-start | bytes 1732
  160.7 9.1 %copy-start.18 = (f32[12,12]{1,0:T(8,128)S(1)}, f32[12,12]{1,0:T(8,128)}, u32[]{:S(2)}) copy-start(f32[12,12]{1,0:T(8,128)} %convolution_bitcast_fusion.6) | copy-start | bytes 1732
  160.7 9.1 %copy-start.19 = (f32[12,12]{1,0:T(8,128)S(1)}, f32[12,12]{1,0:T(8,128)}, u32[]{:S(2)}) copy-start(f32[12,12]{1,0:T(8,128)} %convolution_bitcast_fusion.8) | copy-start | bytes 1732
  160.7 9.1 %copy-start.20 = (f32[12,12]{1,0:T(8,128)S(1)}, f32[12,12]{1,0:T(8,128)}, u32[]{:S(2)}) copy-start(f32[12,12]{1,0:T(8,128)} %convolution_bitcast_fusion.5) | copy-start | bytes 1732
  162.1 16.0 %collective-permute-start.8 = (f32[12,3,1,9,128]{4,0,3,2,1:T(8,128)S(1)}, f32[12,3,1,9,128]{4,0,3,2,1:T(8,128)S(1)}, u32[]{:S(2)}, u32[]{:S(2)}) collective-permute-start(f32[12,3,1,9,128]{4,0,3,2,1:T(8,128)S(1)} %copy.646), channel_id=1, source_target_pairs={{0,4},{4,8},{8,12},{1,5},{5,9},{9,13},{2,6},{6,10},{10,14},{3,7},{... | collective-permute-start | bytes 497672 | tf_op jit(solution)/shard_map/ppermute | solution.py:33
  178.2 5.1 %collective-permute-start.9 = (f32[12,3,2,1,128]{4,0,3,2,1:T(8,128)S(1)}, f32[12,3,2,1,128]{4,0,3,2,1:T(8,128)S(1)}, u32[]{:S(2)}, u32[]{:S(2)}) collective-permute-start(f32[12,3,2,1,128]{4,0,3,2,1:T(8,128)S(1)} %pad_maximum_fusion.7), channel_id=1, source_target_pairs={{0,1},{1,2},{2,3},{4,5},{5,6},{6,7},{8,9},{9,10},{10,11},{12,13},{... | collective-permute-start | bytes 110600 | tf_op jit(solution)/shard_map/ppermute | solution.py:33
  183.4 2.0 copy-start.12
  183.4 2.0 copy-start.13
  (10 other events, 18.3 us)
Sparse Core Ops, SparseCore 0:
  169.8 7.2 reduce-scatter.3
